TPU v7x, 512 devices: a whole 4x8x8 slice. The times are simulated.
512 devices in a mesh: vox: 64 (over x, y, core), grp: 8 (over z).
Axes of the slice: x: 4, y: 8, z: 8, core: 2. Of those that a mesh axis runs over, the one named last changes fastest.
Arguments:
- source_field: bfloat16 [1024, 65536], P(None, 'vox'), may hold values from -4 to 4
- detector_field: bfloat16 [1024, 65536], P(None, 'vox'), may hold values from -4 to 4
- active_block_pairs: int32 [256, 2], P('grp'), may hold values from 0 to 15, as said below
- measurement_counts: int32 [256], P('grp'), may hold values from 1 to 64
- measurement_residual: bfloat16 [256, 4096], P('grp'), may hold values from -6 to 6
Outputs:
- update: float32 [128, 512], P('vox')
- residual: float32 [128, 512], P('vox')
Inputs may be any that keep to these rules, and one draw needn't show every extreme that they name: `active_block_pairs`: each row names a source block below 16 and a detector block below 16; no pair of blocks appears twice.
All inputs are finite; a program needn't handle non-finite values.
Results may differ from a plain program's by a relative error of at most 0.025.
Values may be sent and summed in bfloat16 or wider, within the bound.
A program may use at most 64 MiB of HBM per device.

v0:
```python
import math

import jax
import jax.numpy as jnp
from jax import lax
from jax.sharding import PartitionSpec as P

BLOCK_WIDTH = 64
NY = 32
NZ = 16
ITERS = 2


reg_weight = 0.1


def extended(block, sides, width):
    for axis, dim in sides:
        count = lax.axis_size(axis)
        forward = [(i, i + 1) for i in range(count - 1)]
        backward = [(target, source) for source, target in forward]
        low = lax.ppermute(
            lax.slice_in_dim(block, block.shape[dim] - width, None, axis=dim), axis, forward
        )
        high = lax.ppermute(lax.slice_in_dim(block, 0, width, axis=dim), axis, backward)
        block = jnp.concatenate([low, block, high], axis=dim)
    return block


def gather_blocks(whole_field, block_ids):
    stacked = whole_field.reshape(
        whole_field.shape[0] // BLOCK_WIDTH, BLOCK_WIDTH, whole_field.shape[1]
    )
    return jnp.take(stacked, block_ids, axis=0)


def laplace_term(voxel_field):
    padded = extended(voxel_field, (("vox", 0),), 1)
    grid_cube = padded.reshape(padded.shape[0], NY, NZ)
    centre_cells = grid_cube[1:-1]
    beside = grid_cube[2:] + grid_cube[:-2]
    padded_y = jnp.pad(centre_cells, ((0, 0), (1, 1), (0, 0)))
    beside = beside + padded_y[:, 2:] + padded_y[:, :-2]
    padded_z = jnp.pad(centre_cells, ((0, 0), (0, 0), (1, 1)))
    beside = beside + padded_z[:, :, 2:] + padded_z[:, :, :-2]
    return (7.0 * centre_cells - beside).reshape(voxel_field.shape)


def on_device(
    source_field, detector_field, active_block_pairs, measurement_counts, measurement_residual
):
    pair_count = active_block_pairs.shape[0]
    norm_factor = 1.0 / math.sqrt(pair_count * lax.axis_size("grp") * BLOCK_WIDTH * BLOCK_WIDTH)
    source_rows = gather_blocks(source_field, active_block_pairs[:, 0])
    detect_rows = gather_blocks(detector_field, active_block_pairs[:, 1])
    column_entry = (
        lax.broadcasted_iota(jnp.int32, (pair_count, BLOCK_WIDTH * BLOCK_WIDTH), 1) % BLOCK_WIDTH
    )
    measurement_mask = (column_entry < measurement_counts[:, None]).astype(jnp.float32)

    def project_backward(weights):
        folded = weights.reshape(pair_count, BLOCK_WIDTH, BLOCK_WIDTH)
        spread = jnp.einsum("pbd,pdv->pbv", folded, detect_rows, preferred_element_type=jnp.float32)
        local_sum = norm_factor * jnp.sum(source_rows * spread, axis=(0, 1))
        combined = lax.psum(local_sum, "grp")
        return combined.reshape(-1, NY * NZ)

    def squares(vector):
        return lax.psum(jnp.sum(vector * vector), "vox")

    right_hand_side = project_backward(
        (measurement_mask * measurement_residual).astype(jnp.bfloat16)
    )
    update = jnp.zeros_like(right_hand_side)
    residual = right_hand_side
    direction = right_hand_side
    norm_now = squares(residual)
    for iteration in range(ITERS):
        flattened = direction.reshape(-1)
        scaled = (source_rows * flattened[None, None, :]).astype(jnp.bfloat16)
        partial_value = jnp.einsum(
            "pbv,pdv->pbd", scaled, detect_rows, preferred_element_type=jnp.float32
        )
        partial_value = norm_factor * partial_value.reshape(pair_count, BLOCK_WIDTH * BLOCK_WIDTH)
        summed = lax.psum(partial_value, "vox")
        applied = project_backward(
            (measurement_mask * summed).astype(jnp.bfloat16)
        ) + reg_weight * laplace_term(direction)
        step_length = norm_now / lax.psum(jnp.sum(direction * applied), "vox")
        update = update + step_length * direction
        residual = residual - step_length * applied
        if iteration + 1 < ITERS:
            norm_next = squares(residual)
            direction = residual + norm_next / norm_now * direction
            norm_now = norm_next
    return (update, residual)


def solution(mesh):
    return jax.shard_map(
        on_device,
        mesh=mesh,
        in_specs=(P(None, "vox"), P(None, "vox"), P("grp", None), P("grp"), P("grp", None)),
        out_specs=(P("vox", None), P("vox", None)),
        check_vma=False,
    )
```

profile of v0, /device:TPU:1, one launch (start us, length us, event | category | flops | bytes accessed | tf_op | source)
XLA Modules:
  0.0 990.4 jit_solution(3630918398305233633)
XLA Ops:
  0.7 0.8 compare_and_fusion
  1.5 1.1 select_convert_fusion.2
  2.6 0.5 reshape.84
  3.2 2.7 gather_fusion
  5.9 4.4 gather_fusion.1
  10.3 5.0 fusion
  15.3 20.3 %psum.63 = f32[1024]{0:T(1024)S(1)} all-reduce(f32[1024]{0:T(1024)S(1)} %broadcast_multiply_fusion.2), channel_id=1, replica_groups=mesh['vox'=64,'grp'=8] {'grp'}, use_global_device_ids=true, to_apply=%region_1.3 | all-reduce | flops 1024 | bytes 8192 | tf_op jit(solution)/shard_map/psum | solution.py:65
  35.6 6.3 collective-permute-start
  41.9 3.1 collective-permute-start.1
  45.0 6.0 fusion.11
  51.1 1.6 mul.160
  52.6 247.3 %all-reduce.7 = bf16[32,4096]{1,0:T(8,128)(2,1)S(1)} all-reduce(f32[32,4096]{1,0:T(8,128)S(1)} %mul.160), channel_id=1, replica_groups=mesh['vox'=64,'grp'=8] {'vox'}, use_global_device_ids=true, to_apply=%region_4.6 | all-reduce | flops 131072 | bytes 786432 | tf_op jit(solution)/shard_map/psum | solution.py:85
  299.9 0.1 select_convert_fusion.1
  300.1 0.5 reshape.86
  300.6 5.0 fusion.2
  305.6 10.7 %psum.66 = f32[1024]{0:T(1024)S(1)} all-reduce(f32[1024]{0:T(1024)S(1)} %broadcast_multiply_fusion.1), channel_id=1, replica_groups=mesh['vox'=64,'grp'=8] {'grp'}, use_global_device_ids=true, to_apply=%region_6.8 | all-reduce | flops 1024 | bytes 8192 | tf_op jit(solution)/shard_map/psum | solution.py:65
  316.8 0.6 multiply_reduce_fusion.2
  317.4 133.2 %all-reduce.4 = (f32[]{:T(128)}, f32[]{:T(128)}) all-reduce(f32[]{:T(128)} %get-tuple-element.4, f32[]{:T(128)} %get-tuple-element.3), channel_id=1, replica_groups=mesh['vox'=64,'grp'=8] {'vox'}, use_global_device_ids=true, to_apply=%region_3.5 | all-reduce | flops 2 | bytes 16 | tf_op jit(solution)/shard_map/psum | solution.py:69
  451.9 0.6 multiply_reduce_fusion.1
  452.6 124.7 %psum.68 = f32[]{:T(128)} all-reduce(f32[]{:T(128)} %multiply_reduce_fusion.1), channel_id=1, replica_groups=mesh['vox'=64,'grp'=8] {'vox'}, use_global_device_ids=true, to_apply=%region_10.12 | all-reduce | flops 1 | bytes 8 | tf_op jit(solution)/shard_map/psum | solution.py:69
  578.7 2.6 collective-permute-start.2
  581.2 3.0 collective-permute-start.3
  584.3 6.0 fusion.14
  590.3 1.6 mul.178
  591.9 244.0 %all-reduce.8 = bf16[32,4096]{1,0:T(8,128)(2,1)S(1)} all-reduce(f32[32,4096]{1,0:T(8,128)S(1)} %mul.178), channel_id=1, replica_groups=mesh['vox'=64,'grp'=8] {'vox'}, use_global_device_ids=true, to_apply=%region_11.13 | all-reduce | flops 131072 | bytes 786432 | tf_op jit(solution)/shard_map/psum | solution.py:85
  835.9 0.1 select_convert_fusion
  836.0 0.5 reshape.88
  836.6 5.0 fusion.4
  841.6 12.4 %psum.70 = f32[1024]{0:T(1024)S(1)} all-reduce(f32[1024]{0:T(1024)S(1)} %broadcast_multiply_fusion), channel_id=1, replica_groups=mesh['vox'=64,'grp'=8] {'grp'}, use_global_device_ids=true, to_apply=%region_13.15 | all-reduce | flops 1024 | bytes 8192 | tf_op jit(solution)/shard_map/psum | solution.py:65
  854.3 0.6 multiply_reduce_fusion
  855.0 133.5 %psum.71 = f32[]{:T(128)} all-reduce(f32[]{:T(128)} %multiply_reduce_fusion), channel_id=1, replica_groups=mesh['vox'=64,'grp'=8] {'vox'}, use_global_device_ids=true, to_apply=%region_15.17 | all-reduce | flops 1 | bytes 8 | tf_op jit(solution)/shard_map/psum | solution.py:89
  989.8 0.6 multiply_subtract_fusion
  (34 shorter events, 1.0 us)
Async XLA Ops:
  0.6 2.5 copy-start
  35.6 280.9 %collective-permute-start = (f32[1,512]{1,0:T(1,128)S(1)}, f32[1,512]{1,0:T(1,128)S(1)}, u32[]{:S(2)}, u32[]{:S(2)}) collective-permute-start(f32[1,512]{1,0:T(1,128)S(1)} %bitcast.16), channel_id=1, source_target_pairs={{8,0},{16,8},{24,16},{32,24},{40,32},{48,40},{56,48},{64,56},{72,6... | collective-permute-start | bytes 6152 | tf_op jit(solution)/shard_map/ppermute | solution.py:25
  41.9 258.0 %copy-start.1 = (s32[32]{0:T(128)S(1)}, s32[32]{0:T(128)}, u32[]{:S(2)}) copy-start(s32[32]{0:T(128)} %param.10) | copy-start | bytes 388
  41.9 274.6 %collective-permute-start.1 = (f32[1,512]{1,0:T(1,128)S(1)}, f32[1,512]{1,0:T(1,128)S(1)}, u32[]{:S(2)}, u32[]{:S(2)}) collective-permute-start(f32[1,512]{1,0:T(1,128)S(1)} %bitcast.15), channel_id=1, source_target_pairs={{0,8},{8,16},{16,24},{24,32},{32,40},{40,48},{48,56},{56,64},{64,7... | collective-permute-start | bytes 6152 | tf_op jit(solution)/shard_map/ppermute | solution.py:22
  578.7 275.3 %collective-permute-start.2 = (f32[1,512]{1,0:T(1,128)S(1)}, f32[1,512]{1,0:T(1,128)S(1)}, u32[]{:S(2)}, u32[]{:S(2)}) collective-permute-start(f32[1,512]{1,0:T(1,128)S(1)} %get-tuple-element.14), channel_id=1, source_target_pairs={{8,0},{16,8},{24,16},{32,24},{40,32},{48,40},{56,48},{64,56},{72,6... | collective-permute-start | bytes 6152 | tf_op jit(solution)/shard_map/ppermute | solution.py:25
  581.2 272.8 %collective-permute-start.3 = (f32[1,512]{1,0:T(1,128)S(1)}, f32[1,512]{1,0:T(1,128)S(1)}, u32[]{:S(2)}, u32[]{:S(2)}) collective-permute-start(f32[1,512]{1,0:T(1,128)S(1)} %get-tuple-element.15), channel_id=1, source_target_pairs={{0,8},{8,16},{16,24},{24,32},{32,40},{40,48},{48,56},{56,64},{64,7... | collective-permute-start | bytes 6152 | tf_op jit(solution)/shard_map/ppermute | solution.py:22
where the time goes:
time: 991 us; the launch traced here: 990 us
  blocking collectives  926 us (93%)
  matrix products  27.1 us (3%)
  starting transfers between devices  15 us (2%)
  local copies, waits for them, and re-layouts  12.6 us (1%)
    psum x2, blocking collectives, on_device(): summed = lax.psum(partial_value, 'vox')  491 us
    psum x2, blocking collectives, squares(): return lax.psum(jnp.sum(vector * vector), 'vox')  258 us
    psum x1, blocking collectives, on_device(): step_length = norm_now / lax.psum(jnp.sum(direction * applied), 'vox')  133 us
    psum x3, blocking collectives, project_backward(): combined = lax.psum(local_sum, 'grp')  43.4 us
  transfers between devices with their start and end apart: 4, of which 0 were waited for; matrix products, arithmetic and copies ran while one was open for 3% of the time, Pallas kernels for 0%

commit v1 on v0

v1 whole, which is shorter than its diff:
```python
import functools

import jax
import jax.numpy as jnp
from jax import lax
from jax.experimental import pallas as pl
from jax.experimental.pallas import tpu as pltpu
from jax.sharding import PartitionSpec as P

MESH = pl.DeviceIdType.MESH
F32 = jnp.float32
BF16 = jnp.bfloat16

BLOCK = 64
NORM = 1.0 / 1024.0
REG = 0.1
CHIPS = 32
PLANES = 8
PAIRS = 32


def dot_nt(a, b):
    return lax.dot_general(a, b, (((1,), (1,)), ((), ())), preferred_element_type=F32)


def dot_nn(a, b):
    return lax.dot_general(a, b, (((1,), (0,)), ((), ())), preferred_element_type=F32)


def lane_sum(row):
    return jnp.sum(row, axis=1, keepdims=True)


def fold_rows(acc):
    out = []
    for j in range(8):
        out.append(jnp.sum(acc[:, j * 128 : (j + 1) * 128], axis=0, keepdims=True))
    return NORM * jnp.concatenate(out, axis=0)


def right_side_kernel(pairs, counts, s_ref, d_ref, r_ref, back, zrow, acc):
    vox = lax.axis_index("vox")
    m = vox // 2
    c = vox % 2
    row8 = lax.broadcasted_iota(jnp.int32, (8, 128), 0)
    lane8 = lax.broadcasted_iota(jnp.int32, (8, 128), 1)

    t_own = c * 8 + (m % 4) * 2 + lane8 // BLOCK
    s_own = 2 * row8 + m // 16

    def add_count(p, total):
        hit = (s_own == pairs[p, 0]) & (t_own == pairs[p, 1])
        return total + jnp.where(hit, counts[p].astype(F32), 0.0)

    count_rows = lax.fori_loop(0, PAIRS, add_count, jnp.zeros((8, 128), F32))
    for z in range(PLANES):
        zrow[z] = count_rows[z : z + 1, :]

    lane64 = lax.broadcasted_iota(jnp.int32, (BLOCK, 128), 1)
    acc[...] = jnp.zeros_like(acc)

    def four_pairs(q, carry):
        ids = [4 * q + i for i in range(4)]
        zero = jnp.zeros((BLOCK, 128), BF16)
        rows = []
        for half in range(2):
            low, high = counts[ids[2 * half]], counts[ids[2 * half + 1]]
            block = r_ref[2 * q + half].astype(F32)
            keep_low = lane64 < low
            keep_high = (lane64 >= BLOCK) & (lane64 - BLOCK < high)
            low_part = jnp.where(keep_low & (lane64 < BLOCK), block, 0.0).astype(BF16)
            high_part = jnp.where(keep_high, block, 0.0).astype(BF16)
            for part in (low_part, high_part):
                rows.append(jnp.concatenate([part, zero] if half == 0 else [zero, part], axis=1))
        lhs = jnp.concatenate(rows, axis=0)
        s_at = [pl.multiple_of(pairs[i, 0] * BLOCK, BLOCK) for i in ids]
        t_at = [pl.multiple_of(pairs[i, 1] * BLOCK, BLOCK) for i in ids]
        for n in range(4):
            cols = slice(n * 256, (n + 1) * 256)
            rhs = jnp.concatenate([d_ref[pl.ds(at, BLOCK), cols] for at in t_at], axis=0)
            src = jnp.concatenate([s_ref[pl.ds(at, BLOCK), cols] for at in s_at], axis=0)
            prod = dot_nn(lhs, rhs) * src.astype(F32)
            acc[:, cols] += jnp.sum(prod.reshape(32, 8, 256), axis=0)
        return carry

    lax.fori_loop(0, PAIRS // 4, four_pairs, 0)

    back[...] = fold_rows(acc)


def step_kernel(
    s_ref, d_ref, b_part, zrow,
    upd, res,
    scaled, acc, psend, prcv, pown, xsend, rs, w_all,
    vbuf, halo, csc_snd, csc_rcv, sc_snd, sc_rcv, zbuf, zsm,
    halo_s, halo_r, core_s, core_r, csc_s, csc_r, rs_s, rs_r, sc_s, sc_r,
    ag_s, ag_r, cw_s, cw_r, z_s, z_r, zsm_s, zsm_r,
):
    vox = lax.axis_index("vox")
    g = lax.axis_index("grp")
    m = vox // 2
    c = vox % 2
    partner = (vox + 1 - 2 * c, g)
    up = ((vox + 1) % 64, g)
    down = ((vox + 63) % 64, g)
    cross = ((vox + 63 + 2 * c) % 64, g)

    barrier = pltpu.get_barrier_semaphore()

    def chip_peer(k):
        return (m + k) % CHIPS

    def chip_device(peer):
        return (peer * 2 + c, g)

    def greet_chip(k, carry):
        pl.semaphore_signal(barrier, inc=1, device_id=chip_device(chip_peer(k)), device_id_type=MESH)
        return carry

    def greet_plane(k, carry):
        pl.semaphore_signal(barrier, inc=1, device_id=(vox, (g + k) % PLANES), device_id_type=MESH)
        return carry

    lax.fori_loop(1, PLANES, greet_plane, 0)
    pl.semaphore_signal(barrier, inc=1, device_id=partner, device_id_type=MESH)
    pl.semaphore_signal(barrier, inc=1, device_id=cross, device_id_type=MESH)
    lax.fori_loop(1, CHIPS, greet_chip, 0)

    def remote(src, dst, send, recv, device):
        return pltpu.make_async_remote_copy(
            src_ref=src, dst_ref=dst, send_sem=send, recv_sem=recv,
            device_id=device, device_id_type=MESH,
        )

    def drain(ref, sem):
        pltpu.make_async_copy(ref, ref, sem).wait()

    row8 = lax.broadcasted_iota(jnp.int32, (8, 128), 0)
    lane8 = lax.broadcasted_iota(jnp.int32, (8, 128), 1)

    pl.semaphore_wait(barrier, CHIPS - 1 + PLANES - 1 + 2)

    def plane_sum(phase, part, per_target):
        zbuf[phase, g] = part
        if per_target:
            zsm[phase, g] = zrow[g]

        def send(k, carry):
            peer = (g + k) % PLANES
            device = (vox, peer)
            mine = zbuf.at[phase, g]
            remote(mine, mine, z_s.at[phase], z_r.at[phase], device).start()
            small = zrow.at[peer] if per_target else zsm.at[phase, g]
            remote(small, zsm.at[phase, g], zsm_s.at[phase], zsm_r.at[phase], device).start()
            return carry

        lax.fori_loop(1, PLANES, send, 0)
        drain(zbuf.at[phase, pl.ds(0, PLANES - 1)], z_r.at[phase])
        drain(zsm.at[phase, pl.ds(0, PLANES - 1)], zsm_r.at[phase])
        return jnp.sum(zbuf[phase], axis=0), jnp.sum(zsm[phase], axis=0)

    def laplace(v, low, high):
        low = jnp.where(vox > 0, low, 0.0)
        high = jnp.where(vox < 63, high, 0.0)
        x_m = jnp.where(row8 < 4, pltpu.roll(low, 4, 0), pltpu.roll(v, 4, 0))
        x_p = jnp.where(row8 < 4, pltpu.roll(v, 4, 0), pltpu.roll(high, 4, 0))
        back = pltpu.roll(v, 16, 1)
        ahead = pltpu.roll(v, 112, 1)
        y_m = jnp.where(lane8 >= 16, back, jnp.where(row8 % 4 != 0, pltpu.roll(back, 1, 0), 0.0))
        y_p = jnp.where(lane8 < 112, ahead, jnp.where(row8 % 4 != 3, pltpu.roll(ahead, 7, 0), 0.0))
        z_m = jnp.where(lane8 % 16 != 0, pltpu.roll(v, 1, 1), 0.0)
        z_p = jnp.where(lane8 % 16 != 15, pltpu.roll(v, 127, 1), 0.0)
        return 7.0 * v - (x_m + x_p + y_m + y_p + z_m + z_p)

    s_rows = pl.ds(pl.multiple_of(g * 128, 128), 128)
    lt_own = m % 4
    row_own = pl.multiple_of((m // 4) * 16, 16)

    def forward(it, v, scalar_terms):
        vbuf[it] = v
        to_up = remote(vbuf.at[it], halo.at[it, 0], halo_s.at[it, 0], halo_r.at[it, 0], up)
        to_down = remote(vbuf.at[it], halo.at[it, 1], halo_s.at[it, 1], halo_r.at[it, 1], down)
        to_up.start()
        to_down.start()
        for j in range(8):
            cols = slice(j * 128, (j + 1) * 128)
            scaled[:, cols] = (s_ref[s_rows, cols].astype(F32) * v[j : j + 1, :]).astype(BF16)

        def half(side, n):
            start = pl.multiple_of(side * 512 + n * 256, 256)
            return dot_nt(scaled[...], d_ref[pl.ds(start, 256), :])

        for n in range(2):
            part = half(1 - c, n).astype(BF16)
            psend[it, 2 * n] = part[:, :128]
            psend[it, 2 * n + 1] = part[:, 128:]
        to_core = remote(psend.at[it], prcv.at[it], core_s.at[it], core_r.at[it], partner)
        to_core.start()

        to_up.wait()
        to_down.wait()
        lap = laplace(v, halo[it, 0], halo[it, 1])
        terms = scalar_terms(lap)
        packed = jnp.zeros((1, 128), F32)
        lane1 = lax.broadcasted_iota(jnp.int32, (1, 128), 1)
        for i, term in enumerate(terms):
            packed += jnp.where(lane1 == i, lane_sum(jnp.sum(term, axis=0, keepdims=True)), 0.0)
        csc_snd[it] = packed
        to_core_sc = remote(csc_snd.at[it], csc_rcv.at[it], csc_s.at[it], csc_r.at[it], partner)
        to_core_sc.start()

        for n in range(2):
            part = half(c, n)
            pown[2 * n] = part[:, :128]
            pown[2 * n + 1] = part[:, 128:]
        to_core.wait()
        for lt in range(4):
            total = pown[lt] + prcv[it, lt].astype(F32)
            pown[lt] = total
            xsend[it, lt] = total.astype(BF16)

        def scatter(k, carry):
            peer = chip_peer(k)
            src = xsend.at[it, peer % 4, pl.ds(pl.multiple_of((peer // 4) * 16, 16), 16), :]
            remote(src, rs.at[it, k - 1], rs_s.at[it], rs_r.at[it], chip_device(peer)).start()
            return carry

        lax.fori_loop(1, CHIPS, scatter, 0)

        to_core_sc.wait()
        mine = packed + csc_rcv[it]
        sc_snd[it] = mine

        def scatter_sc(k, carry):
            remote(
                sc_snd.at[it], sc_rcv.at[it, k - 1], sc_s.at[it], sc_r.at[it], chip_device(chip_peer(k))
            ).start()
            return carry

        lax.fori_loop(1, CHIPS, scatter_sc, 0)
        drain(rs.at[it], rs_r.at[it])
        total = pown[lt_own, pl.ds(row_own, 16), :] + jnp.sum(rs[it].astype(F32), axis=0)
        drain(sc_rcv.at[it], sc_r.at[it])
        sums = mine + jnp.sum(sc_rcv[it], axis=0)
        scalars = [lane_sum(jnp.where(lane1 == i, sums, 0.0)) for i in range(len(terms))]
        return NORM * total, scalars, lap

    def backward(it, weights):
        chunk = w_all.at[it, c * 4 + lt_own, pl.ds(row_own, 16), :]
        chunk[...] = weights

        def gather(k, carry):
            remote(chunk, chunk, ag_s.at[it], ag_r.at[it], chip_device(chip_peer(k))).start()
            return carry

        lax.fori_loop(1, CHIPS, gather, 0)
        drain(rs.at[it], ag_r.at[it])
        own_half = w_all.at[it, pl.ds(c * 4, 4)]
        to_core = remote(own_half, own_half, cw_s.at[it], cw_r.at[it], partner)
        to_core.start()
        acc[...] = jnp.zeros_like(acc)

        def use(side):
            tiles = w_all[it, pl.ds(side * 4, 4)]
            lhs = jnp.concatenate([tiles[i] for i in range(4)], axis=1)
            rows = pl.ds(pl.multiple_of(side * 512, 512), 512)
            for n in range(4):
                cols = slice(n * 256, (n + 1) * 256)
                prod = dot_nn(lhs, d_ref[rows, cols]) * s_ref[s_rows, cols].astype(F32)
                acc[:, cols] += jnp.sum(prod.reshape(16, 8, 256), axis=0)
            wide = tiles.astype(F32)
            return jnp.sum((wide * wide).reshape(64, 8, 128), axis=0)

        ww = use(c)
        to_core.wait()
        ww = ww + use(1 - c)
        zsm[it + 1, g] = jnp.sum(ww, axis=0, keepdims=True)
        back, ww_row = plane_sum(it + 1, fold_rows(acc), False)
        return back, lane_sum(ww_row)

    b, count_row = plane_sum(0, b_part[...], True)
    lane16 = lax.broadcasted_iota(jnp.int32, (16, 128), 1)
    keep = (lane16 % BLOCK).astype(F32) < count_row

    def masked(values):
        return jnp.where(keep, values, 0.0).astype(BF16)

    jd0, (rr0, dld0), lap_b = forward(0, b, lambda lap: [b * b, b * lap])
    back0, ww0 = backward(0, masked(jd0))
    alpha0 = rr0 / (ww0 + REG * dld0)
    x1 = alpha0 * b
    r1 = b - alpha0 * (back0 + REG * lap_b)

    jr1, (rr1, rlr, rld), lap_r = forward(1, r1, lambda lap: [r1 * r1, r1 * lap, r1 * lap_b])
    beta = rr1 / rr0
    back1, ww1 = backward(1, masked(jr1 + beta * jd0))
    dld1 = rlr + 2.0 * beta * rld + beta * beta * dld0
    alpha1 = rr1 / (ww1 + REG * dld1)
    d1 = r1 + beta * b
    x2 = x1 + alpha1 * d1
    r2 = r1 - alpha1 * (back1 + REG * (lap_r + beta * lap_b))
    for j in range(8):
        cols = slice((j % 4) * 128, (j % 4 + 1) * 128)
        upd[j // 4 : j // 4 + 1, cols] = x2[j : j + 1, :]
        res[j // 4 : j // 4 + 1, cols] = r2[j : j + 1, :]

    for it in range(2):
        drain(rs.at[it], rs_s.at[it])
        drain(rs.at[it], ag_s.at[it])
        drain(sc_rcv.at[it], sc_s.at[it])
    for phase in range(3):
        drain(zbuf.at[phase, pl.ds(0, PLANES - 1)], z_s.at[phase])
        drain(zsm.at[phase, pl.ds(0, PLANES - 1)], zsm_s.at[phase])


def on_device(source_field, detector_field, active_block_pairs, measurement_counts, measurement_residual):
    blocks = measurement_residual.reshape(PAIRS // 2, 2, BLOCK, BLOCK).transpose(0, 2, 1, 3)
    blocks = blocks.reshape(PAIRS // 2, BLOCK, 2 * BLOCK)
    dma = pltpu.SemaphoreType.DMA
    vmem = pltpu.VMEM
    out = jax.ShapeDtypeStruct((2, 512), F32)
    on_chip = pl.BlockSpec(memory_space=pltpu.VMEM)
    b_part, count_rows = pl.pallas_call(
        right_side_kernel,
        out_shape=(jax.ShapeDtypeStruct((8, 128), F32), jax.ShapeDtypeStruct((PLANES, 1, 128), F32)),
        in_specs=[pl.BlockSpec(memory_space=pltpu.SMEM)] * 2 + [on_chip] * 3,
        out_specs=(on_chip,) * 2,
        scratch_shapes=[vmem((8, 1024), F32)],
        compiler_params=pltpu.CompilerParams(vmem_limit_bytes=24 * 1024 * 1024),
    )(active_block_pairs, measurement_counts, source_field, detector_field, blocks)
    return pl.pallas_call(
        step_kernel,
        out_shape=(out, out),
        in_specs=[on_chip] * 4,
        out_specs=(on_chip,) * 2,
        scratch_shapes=[
            vmem((128, 1024), BF16),
            vmem((8, 1024), F32),
            vmem((2, 4, 128, 128), BF16),
            vmem((2, 4, 128, 128), BF16),
            vmem((4, 128, 128), F32),
            vmem((2, 4, 128, 128), BF16),
            vmem((2, CHIPS - 1, 16, 128), BF16),
            vmem((2, 8, 128, 128), BF16),
            vmem((2, 8, 128), F32),
            vmem((2, 2, 8, 128), F32),
            vmem((2, 1, 128), F32),
            vmem((2, 1, 128), F32),
            vmem((2, 1, 128), F32),
            vmem((2, CHIPS - 1, 1, 128), F32),
            vmem((3, PLANES, 8, 128), F32),
            vmem((3, PLANES, 1, 128), F32),
            dma((2, 2)), dma((2, 2)),
            dma((2,)), dma((2,)),
            dma((2,)), dma((2,)),
            dma((2,)), dma((2,)),
            dma((2,)), dma((2,)),
            dma((2,)), dma((2,)),
            dma((2,)), dma((2,)),
            dma((3,)), dma((3,)),
            dma((3,)), dma((3,)),
        ],
        compiler_params=pltpu.CompilerParams(
            collective_id=0, has_side_effects=True, vmem_limit_bytes=24 * 1024 * 1024
        ),
    )(source_field, detector_field, b_part, count_rows)


def solution(mesh):
    return jax.shard_map(
        on_device,
        mesh=mesh,
        in_specs=(P(None, "vox"), P(None, "vox"), P("grp", None), P("grp"), P("grp", None)),
        out_specs=(P("vox", None), P("vox", None)),
        check_vma=False,
    )
```

time: 991 us -> 79.7 us (0.08)
  blocking collectives: 926 us -> 0 us
  Pallas kernels: 0 us -> 73.6 us
  matrix products: 27.1 us -> 0 us
  starting transfers between devices: 15 us -> 0 us
    psum x8 -> x0, blocking collectives: 926 us -> none  [the longest x2 491 us: on_device(): summed = lax.psum(partial_value, 'vox')]
    pallas_call x0 -> x2, Pallas kernels: none -> 73.6 us  [the longest x1 70 us: on_device(): pl.pallas_call(step_kernel, out_shape=(out, out), in_specs=[on_chip] * 4,...]
    dot_general x5 -> x0, matrix products: 27.1 us -> none  [the longest x3 15 us: project_backward(): jnp.einsum('pbd,pdv->pbv', folded, detect_rows, preferred_element_type=jn...]
    ppermute x4 -> x0, starting transfers between devices: 15 us -> none  [the longest x2 8.89 us: extended(): lax.ppermute(lax.slice_in_dim(block, 0, width, axis=dim), axis, backward)]
  transfers between devices with their start and end apart: 4 -> 0, of which waited for: 0 -> 0; matrix products, arithmetic and copies ran while one was open for 3% -> 0% of each run, Pallas kernels for 0% -> 0%
where the time goes in v1:
time: 79.7 us; the launch traced here: 79.6 us
  Pallas kernels  73.6 us (92%)
  local copies, waits for them, and re-layouts  5.3 us (7%)
    pallas_call x1, Pallas kernels, on_device(): pl.pallas_call(step_kernel, out_shape=(out, out), in_specs=[on_chip] * 4,...  70 us
    pallas_call x1, Pallas kernels, on_device(): pl.pallas_call(right_side_kernel, out_shape=(jax.ShapeDtypeStruct((8, 128...  3.54 us
    unnamed x11, local copies, waits for them, and re-layouts  2.88 us
    reshape x2, local copies, waits for them, and re-layouts, on_device(): measurement_residual.reshape(PAIRS // 2, 2, BLOCK, BLOCK)  2.16 us

profile of v1, /device:TPU:1, one launch (start us, length us, event | category | flops | bytes accessed | tf_op | source)
XLA Modules:
  0.0 79.6 jit_solution(5194267208105609500)
XLA Ops:
  0.6 0.0 copy-start.3
  0.6 0.0 copy-start
  0.7 0.0 copy-start.2
  0.7 1.6 %reshape.10 = bf16[16,2,64,64]{3,2,1,0:T(8,128)(2,1)S(1)} reshape(bf16[32,4096]{1,0:T(8,128)(2,1)} %param.9) | data formatting | bytes 524288 | tf_op jit(solution)/shard_map/reshape | solution.py:317
  2.3 0.5 copy.10
  2.8 0.3 reshape.11.r_ref
  3.1 0.0 copy-done.3
  3.1 0.1 copy.8.pairs
  3.2 0.0 copy-done
  3.2 0.0 copy-done.2
  3.2 0.0 copy-start.1
  3.2 1.6 %copy-done.1 = bf16[1024,1024]{1,0:T(8,128)(2,1)S(1)} copy-done((bf16[1024,1024]{1,0:T(8,128)(2,1)S(1)}, bf16[1024,1024]{1,0:T(8,128)(2,1)}, u32[]{:S(2)}) %copy-start.1) | copy-done | bytes 2097176
  4.8 3.5 %shard_map.68 = (f32[8,128]{1,0:T(8,128)S(1)}, f32[8,1,128]{2,1,0:T(1,128)S(1)}) custom-call(s32[32,2]{1,0:T(8,128)S(1)} %copy.8.pairs, s32[32]{0:T(128)S(1)} %copy-done.2, bf16[1024,1024]{1,0:T(8,128)(2,1)S(1)} %copy-done, bf16[1024,1024]{1,0:T(8,128)(2,1)S(1)} %copy-done.1, bf16[16,64,128]{2,1,0:T(8,128)(2,1)S(1)} %reshape.11.r_ref), custom_call_target="tpu_custom_call" | custom-call | tf_op jit(solution)/shard_map/pallas_call | solution.py:323
  8.3 70.0 %shard_map.69 = (f32[2,512]{1,0:T(2,128)S(1)}, f32[2,512]{1,0:T(2,128)S(1)}) custom-call(bf16[1024,1024]{1,0:T(8,128)(2,1)S(1)} %copy-done, bf16[1024,1024]{1,0:T(8,128)(2,1)S(1)} %copy-done.1, f32[8,128]{1,0:T(8,128)S(1)} %get-tuple-element.4.b_part, f32[8,1,128]{2,1,0:T(1,128)S(1)} %get-tuple-element.5.zrow), custom_call_target="tpu_custom_call" | custom-call | tf_op jit(solution)/shard_map/pallas_call | solution.py:331
  78.4 0.6 copy.13
  79.0 0.6 copy.14
Async XLA Ops:
  0.6 2.5 %copy-start.3 = (s32[32,2]{0,1:T(2,128)S(1)}, s32[32,2]{0,1:T(2,128)}, u32[]{:S(2)}) copy-start(s32[32,2]{0,1:T(2,128)} %param.7) | copy-start | bytes 772
  0.6 2.6 %copy-start = (bf16[1024,1024]{1,0:T(8,128)(2,1)S(1)}, bf16[1024,1024]{1,0:T(8,128)(2,1)}, u32[]{:S(2)}) copy-start(bf16[1024,1024]{1,0:T(8,128)(2,1)} %s_ref.3) | copy-start | bytes 6291460
  0.7 2.5 %copy-start.2 = (s32[32]{0:T(128)S(1)}, s32[32]{0:T(128)}, u32[]{:S(2)}) copy-start(s32[32]{0:T(128)} %counts.1) | copy-start | bytes 388
  3.2 1.6 %copy-start.1 = (bf16[1024,1024]{1,0:T(8,128)(2,1)S(1)}, bf16[1024,1024]{1,0:T(8,128)(2,1)}, u32[]{:S(2)}) copy-start(bf16[1024,1024]{1,0:T(8,128)(2,1)} %d_ref.3) | copy-start | bytes 6291460
